TPU v7x, 32 devices: a whole 2x2x4 slice. The times are simulated.
32 devices in a mesh: row: 4 (over z), col: 4 (over y, x), wave: 2 (over core).
Axes of the slice: x: 2, y: 2, z: 4, core: 2. Of those that a mesh axis runs over, the one named last changes fastest.
Arguments:
- transmission: float32 [4096, 4096], P('row', 'col'), may hold values from 0 to 1
- dual_focal: float32 [512, 8, 512], P(('row', 'col'), 'wave'), may hold values from -12 to 12
- dual_curvature: float32 [4096, 4096], P('row', 'col'), may hold values from -6 to 6
- pupil_mask: int32 [4096, 4096], P('row', 'col'), may hold values 0 or 1
- lyot_mask: int32 [4096, 4096], P('row', 'col'), may hold values 0 or 1
- dark_mask: int32 [512, 8, 512], P(('row', 'col'), 'wave'), may hold values 0 or 1
- focal_rows: float32 [8, 512, 4096], P('wave', None, 'row'), may hold values from -0.09375 to 0.09375
- focal_cols: float32 [8, 512, 4096], P('wave', None, 'col'), may hold values from -0.09375 to 0.09375
Outputs:
- transmission_out: float32 [4096, 4096], P('row', 'col')
- dual_focal_out: float32 [512, 8, 512], P(('row', 'col'), 'wave')
- dual_curvature_out: float32 [4096, 4096], P('row', 'col')
All inputs are finite; a program needn't handle non-finite values. No bound on the sum of `pupil_mask` or of `lyot_mask` or of `dark_mask` on one device may be relied on, other than what follows from the above.
Results may differ from a plain program's by a relative error of at most 0.0001.
Values sent between devices are 32-bit elements; how exact they have to be, the bound alone decides.
A program may use at most 128 MiB of HBM per device.

v0:
```python
import types

import jax
import jax.numpy as jnp
from jax import lax
from jax.experimental import pallas as pl
from jax.experimental.pallas import tpu as pltpu
from jax.sharding import PartitionSpec as P

ITERS = 2
step_primal = 0.12
step_dual = 0.2
contrast = 0.5
curvature_limit = 0.1
BLOCK = 128
LIMIT = 61 << 20
MESH = pl.DeviceIdType.MESH
f32, bf16 = jnp.float32, jnp.bfloat16
VMEM = pl.BlockSpec(memory_space=pltpu.VMEM)
ANY = pl.BlockSpec(memory_space=pl.ANY)
DMA = pltpu.SemaphoreType.DMA


def shape(*dims, kind=f32):
    return jax.ShapeDtypeStruct(dims, kind)


def prox(v, limit):
    return v - jnp.clip(v, -step_dual * limit, step_dual * limit)


def stencil(v, up, down, left, right):
    rows, cols = v.shape
    r = lax.broadcasted_iota(jnp.int32, v.shape, 0)
    c = lax.broadcasted_iota(jnp.int32, v.shape, 1)
    from_up = jnp.where(r == 0, up, pltpu.roll(v, 1, 0))
    from_down = jnp.where(r == rows - 1, down, pltpu.roll(v, rows - 1, 0))
    from_left = jnp.where(c == 0, left, pltpu.roll(v, 1, 1))
    from_right = jnp.where(c == cols - 1, right, pltpu.roll(v, cols - 1, 1))
    return 0.25 * (from_down + from_up + from_right + from_left) - v


def column(row):
    n = row.shape[1]
    return jnp.transpose(jnp.broadcast_to(row, (128, n)))[:, 0:1]


class Place:
    def __init__(self):
        self.r, self.c = lax.axis_index("row"), lax.axis_index("col")
        self.nr, self.nc = lax.axis_size("row"), lax.axis_size("col")
        self.na = 2 if self.nc % 2 == 0 else 1
        self.nb = self.nc // self.na
        self.w, self.nw = lax.axis_index("wave"), lax.axis_size("wave")
        self.a, self.b = self.c // self.nb, lax.rem(self.c, self.nb)

    def wave(self, n):
        return {"wave": lax.rem(self.w + n, self.nw)}

    def row(self, d):
        return lax.rem(self.r + d, self.nr)

    def col(self, f, e):
        return lax.rem(self.a + f, self.na) * self.nb + lax.rem(self.b + e, self.nb)

    def greet(self, waves):
        barrier = pltpu.get_barrier_semaphore()
        for d in range(1, self.nr):
            pl.semaphore_signal(barrier, inc=1, device_id={"row": self.row(d)}, device_id_type=MESH)
        for e in range(1, self.nc):
            pl.semaphore_signal(barrier, inc=1, device_id={"col": lax.rem(self.c + e, self.nc)}, device_id_type=MESH)
        peers = self.nr + self.nc - 2
        if waves:
            for n in range(1, self.nw):
                pl.semaphore_signal(barrier, inc=1, device_id=self.wave(n), device_id_type=MESH)
            peers += self.nw - 1
        pl.semaphore_wait(barrier, peers)


def remote(src, dst, sems, index, where):
    return pltpu.make_async_remote_copy(
        src_ref=src, dst_ref=dst, send_sem=sems.at[(0,) + index], recv_sem=sems.at[(1,) + index],
        device_id=where, device_id_type=MESH)


def start(copies):
    for copy in copies:
        copy.start()


def arrived(copies):
    for copy in copies:
        copy.wait_recv()


def sent(copies):
    for copy in copies:
        copy.wait_send()


def each(count, step):
    def body(i, carry):
        step(i)
        return carry

    lax.fori_loop(0, count, body, 0)


class Gather:
    def __init__(self, p, full, sems):
        self.p, self.full = p, full
        self.zs, self.bs, self.as_, self.h0, self.h1 = sems

    @staticmethod
    def scratch(waves, nr, na, nb):
        return [DMA((2, waves, nr)), DMA((2, waves, nr, nb)), DMA((2, waves, nr, na)), DMA((2, waves, na, nb)), DMA((2, waves, na, nb))]

    def along(self, w):
        p = self.p
        own = self.full.at[w, p.r, p.c]
        return [remote(own, own, self.zs, (w, d), {"row": p.row(d)}) for d in range(1, p.nr)]

    def across(self, w, d):
        p = self.p
        block = self.full.at[w, p.row(p.nr - d) if d else p.r, p.c]
        return ([remote(block, block, self.bs, (w, d, e), {"col": p.col(0, e)}) for e in range(1, p.nb)]
                + [remote(block, block, self.as_, (w, d, f), {"col": p.col(f, 0)}) for f in range(1, p.na)])

    def relays(self, w):
        p, out = self.p, []
        half = self.full.shape[-1] // 2
        for e in range(1, p.nb):
            for f in range(1, p.na):
                low = self.full.at[w, :, p.col(0, p.nb - e), :, pl.ds(0, half)]
                out.append(remote(low, low, self.h0, (w, f, e), {"col": p.col(f, 0)}))
                top = self.full.at[w, :, p.col(p.na - f, 0), :, pl.ds(half, half)]
                out.append(remote(top, top, self.h1, (w, f, e), {"col": p.col(0, e)}))
        return out

    def start(self, w):
        start(self.along(w))

    def spread(self, w):
        start(self.across(w, 0))

    def forward(self, w, then=None):
        for d, copy in enumerate(self.along(w), 1):
            copy.wait_recv()
            if d == 1 and then is not None:
                then()
            start(self.across(w, d))

    def relay(self, w):
        for d in range(self.p.nr):
            arrived(self.across(w, d))
        start(self.relays(w))

    def arrive(self, w):
        arrived(self.relays(w))

    def finish(self):
        def step(w):
            sent(self.along(w) + self.relays(w))
            for d in range(self.p.nr):
                sent(self.across(w, d))

        each(self.full.shape[0], step)


class Scatter:
    def __init__(self, p, part, scratch):
        self.p, self.part = p, part
        self.g0, self.g1, self.gb, self.ga, self.q, self.gz = scratch[:6]
        self.s0, self.s1, self.db, self.da, self.rb, self.ra, self.zs = scratch[6:]
        half = part.shape[-1] // 2
        self.low, self.top = pl.ds(0, half), pl.ds(half, half)

    @staticmethod
    def scratch(waves, nr, na, nb, k, z):
        v = lambda *dims: pltpu.VMEM(dims, f32)
        fa, fb = max(na - 1, 1), max(nb - 1, 1)
        return [
            v(waves, fa, fb, nr, k, z // 2), v(waves, fa, fb, nr, k, z // 2),
            v(waves, fb, nr, k, z), v(waves, fa, nr, k, z), v(waves, nr, k, z), v(waves, nr, k, z),
            DMA((2, waves, na, nb)), DMA((2, waves, na, nb)), DMA((2, waves, nb)), DMA((2, waves, na)),
            DMA((2, waves, nb)), DMA((2, waves, na)), DMA((2, waves, nr))]

    def first(self, w):
        p, out = self.p, []
        for f in range(1, p.na):
            for e in range(1, p.nb):
                diagonal = self.part.at[w, :, p.col(f, e)]
                out.append(remote(diagonal.at[:, :, self.low], self.g0.at[w, f - 1, e - 1], self.s0, (w, f, e), {"col": p.col(f, 0)}))
                out.append(remote(diagonal.at[:, :, self.top], self.g1.at[w, f - 1, e - 1], self.s1, (w, f, e), {"col": p.col(0, e)}))
        return out

    def direct(self, w):
        p, low, top = self.p, self.low, self.top
        return ([remote(self.part.at[w, :, p.col(0, e), :, top], self.gb.at[w, e - 1, :, :, top], self.db, (w, e), {"col": p.col(0, e)})
                 for e in range(1, p.nb)]
                + [remote(self.part.at[w, :, p.col(f, 0), :, low], self.ga.at[w, f - 1, :, :, low], self.da, (w, f), {"col": p.col(f, 0)})
                   for f in range(1, p.na)])

    def second(self, w):
        p, low, top = self.p, self.low, self.top
        return ([remote(self.g0.at[w, 0, e - 1], self.gb.at[w, e - 1, :, :, low], self.rb, (w, e), {"col": p.col(0, e)})
                 for e in range(1, p.nb)]
                + [remote(self.g1.at[w, f - 1, 0], self.ga.at[w, f - 1, :, :, top], self.ra, (w, f), {"col": p.col(f, 0)})
                   for f in range(1, p.na)])

    def third(self, w):
        p = self.p
        return [remote(self.q.at[w, p.row(d)], self.gz.at[w, d], self.zs, (w, d), {"row": p.row(d)}) for d in range(1, p.nr)]

    def start(self, w):
        start(self.first(w))

    def combine(self, w):
        p = self.p
        arrived(self.first(w))
        for e in range(1, p.nb):
            total = self.part[w, :, p.col(0, e), :, self.low]
            for f in range(1, p.na):
                total = total + self.g0[w, f - 1, e - 1]
            self.g0[w, 0, e - 1] = total
        for f in range(1, p.na):
            total = self.part[w, :, p.col(f, 0), :, self.top]
            for e in range(1, p.nb):
                total = total + self.g1[w, f - 1, e - 1]
            self.g1[w, f - 1, 0] = total
        start(self.second(w) + self.direct(w))

    def column(self, w):
        p = self.p
        arrived(self.direct(w) + self.second(w))
        total = self.part[w, :, p.c]
        for e in range(1, p.nb):
            total = total + self.gb[w, e - 1]
        for f in range(1, p.na):
            total = total + self.ga[w, f - 1]
        self.q[w] = total
        start(self.third(w))

    def result(self, w):
        arrived(self.third(w))
        total = self.q[w, self.p.r]
        for d in range(1, self.p.nr):
            total = total + self.gz[w, d]
        return total

    def finish(self):
        each(self.part.shape[0], lambda w: sent(self.first(w) + self.direct(w) + self.second(w) + self.third(w)))


class Halo:
    def __init__(self, p, v, scratch):
        self.p, self.v = p, v
        self.packed, self.rows, self.cols, self.sems = scratch

    @staticmethod
    def scratch(rows, cols):
        v = lambda *dims: pltpu.VMEM(dims, f32)
        return [v(2, 8, rows), v(2, 8, cols), v(2, 8, rows), DMA((2, 4))]

    def copies(self):
        p, rows = self.p, self.v.shape[0]
        up, down = {"row": p.row(p.nr - 1)}, {"row": p.row(1)}
        left, right = {"col": lax.rem(p.c + p.nc - 1, p.nc)}, {"col": lax.rem(p.c + 1, p.nc)}
        return [
            remote(self.v.at[pl.ds(rows - 8, 8)], self.rows.at[0], self.sems, (0,), down),
            remote(self.v.at[pl.ds(0, 8)], self.rows.at[1], self.sems, (1,), up),
            remote(self.packed.at[1], self.cols.at[0], self.sems, (2,), right),
            remote(self.packed.at[0], self.cols.at[1], self.sems, (3,), left),
        ]

    def start(self):
        cols = self.v.shape[1]
        self.packed[0] = jnp.transpose(self.v[:, 0:128])[0:8]
        self.packed[1] = jnp.transpose(self.v[:, cols - 128:cols])[120:128]
        start(self.copies())

    def result(self, out_r, out_c):
        p = self.p
        arrived(self.copies())
        out_r[0] = jnp.where(p.r > 0, self.rows[0], 0.0)
        out_r[1] = jnp.where(p.r < p.nr - 1, self.rows[1], 0.0)
        out_c[0] = jnp.where(p.c > 0, self.cols[0], 0.0)
        out_c[1] = jnp.where(p.c < p.nc - 1, self.cols[1], 0.0)

    def finish(self):
        sent(self.copies())


def curvature(v, i, block, edge_r, edge_c):
    rows = v.shape[0]
    at = pl.multiple_of(i * block, block)
    here = pl.ds(at, block)
    above = v[pl.ds(pl.multiple_of(jnp.maximum(at - 8, 0), 8), 8), :][7:8]
    below = v[pl.ds(pl.multiple_of(jnp.minimum(at + block, rows - 8), 8), 8), :][0:1]
    up = jnp.where(i == 0, edge_r[0, 7:8, :], above)
    down = jnp.where(i == rows // block - 1, edge_r[1, 0:1, :], below)
    return stencil(v[here, :], up, down, column(edge_c[0, 7:8, here]), column(edge_c[1, 0:1, here]))


def curvature_step(dual, ext, edge_r, edge_c, lo, hi):
    def step(i, _):
        here = pl.ds(pl.multiple_of(i * BLOCK, BLOCK), BLOCK)
        moved = dual[here, :] + step_dual * curvature(ext, i, BLOCK, edge_r, edge_c)
        dual[here, :] = prox(moved, curvature_limit)
        return 0

    lax.fori_loop(lo, hi, step, 0)


def split(v):
    top = v.astype(bf16)
    return top, (v - top.astype(f32)).astype(bf16)


def dot3(a, b, over):
    def dot(u, v):
        return lax.dot_general(u, v, (over, ((), ())), preferred_element_type=f32)

    return dot(a[0], b[0]) + dot(a[0], b[1]) + dot(a[1], b[0])


def forward_left(m, w):
    u, cols = m.lh.shape
    step = min(512, cols)
    for n in range(cols // step):
        j = pl.ds(n * step, step)
        m.lh[:, j], m.ll[:, j] = split(dot3((m.rh[w], m.rl[w]), (m.ah[:, j], m.al[:, j]), ((1,), (0,))))


def forward_part(m, w):
    out = dot3((m.lh[...], m.ll[...]), (m.ch[w], m.cl[w]), ((1,), (1,)))
    m.part[w] = out.reshape(m.part.shape[1:])


def back_tile(m, w, t, size):
    cols = m.acc.shape[1]
    i = pl.ds(pl.multiple_of(t * size, size), size)
    m.sh[...], m.sl[...] = split(dot3((m.rh[w, :, i], m.rl[w, :, i]), (m.yh[...], m.yl[...]), ((0,), (0,))))
    step = min(512, cols)
    for n in range(cols // step):
        j = pl.ds(n * step, step)
        m.acc[i, j] = m.acc[i, j] + dot3((m.sh[...], m.sl[...]), (m.ch[w, :, j], m.cl[w, :, j]), ((1,), (0,)))


def clear(m):
    def step(i):
        m.acc[pl.ds(pl.multiple_of(i * BLOCK, BLOCK), BLOCK), :] = jnp.zeros((BLOCK, m.acc.shape[1]), f32)

    each(m.acc.shape[0] // BLOCK, step)


class Primal:
    def __init__(self, p, m, x, x_out):
        self.p, self.m, self.x, self.x_out = p, m, x, x_out
        rows = m.acc.shape[0]
        self.size = m.sh.shape[0]
        self.tiles = rows // self.size

    @staticmethod
    def scratch(rows, cols, nw, tile):
        v = lambda *dims: pltpu.VMEM(dims, f32)
        i32 = lambda *dims: pltpu.VMEM(dims, jnp.int32)
        return dict(
            acc=v(rows, cols), other=v(max(nw - 1, 1), rows, cols), wave_sems=DMA((2, rows // tile, nw)),
            x_in=v(2, BLOCK, cols), pupil_in=i32(2, BLOCK, cols), lyot_in=i32(2, BLOCK, cols), in_sems=DMA((2, 3)),
            out_sems=DMA((rows // tile,)))

    def load(self, i, slot):
        m = self.m
        here = pl.ds(pl.multiple_of(i * BLOCK, BLOCK), BLOCK)
        pairs = ((self.x, m.x_in), (m.pupil, m.pupil_in), (m.lyot, m.lyot_in))
        return [pltpu.make_async_copy(a.at[here], b.at[slot], m.in_sems.at[slot, n]) for n, (a, b) in enumerate(pairs)]

    def begin(self):
        for i in range(2):
            for copy in self.load(i, i):
                copy.start()

    def exchange(self, t):
        p, m = self.p, self.m
        here = pl.ds(pl.multiple_of(t * self.size, self.size), self.size)
        return [remote(m.acc.at[here], m.other.at[n - 1, here], m.wave_sems, (t, n), p.wave(n)) for n in range(1, p.nw)]

    def store(self, t):
        m = self.m
        here = pl.ds(pl.multiple_of(t * self.size, self.size), self.size)
        return pltpu.make_async_copy(m.acc.at[here], self.x_out.at[here], m.out_sems.at[t])

    def step(self, i):
        p, m = self.p, self.m
        slot = lax.rem(i, 2)
        here = pl.ds(pl.multiple_of(i * BLOCK, BLOCK), BLOCK)
        for copy in self.load(i, slot):
            copy.wait()
        pupil = m.pupil_in[slot].astype(f32)
        stop = pupil * m.lyot_in[slot].astype(f32)
        x = m.x_in[slot]
        total = m.acc[here, :]
        for n in range(1, p.nw):
            total = total + m.other[n - 1, here, :]
        gradient = stop * total - pupil + curvature(m.dual_v, i, BLOCK, m.dual_r, m.dual_c)
        new = jnp.clip(x - step_primal * gradient, 0.0, 1.0)
        ext = 2.0 * new - x
        m.acc[here, :] = new
        m.ext_v[here, :] = ext
        m.ah[here, :], m.al[here, :] = split(stop * ext)

        @pl.when(i + 2 < m.acc.shape[0] // BLOCK)
        def _():
            for copy in self.load(i + 2, slot):
                copy.start()

    def finish(self):
        per = self.size // BLOCK

        def tile(t):
            for copy in self.exchange(t):
                copy.wait()
            each(per, lambda i: self.step(t * per + i))
            self.store(t).start()

        each(self.tiles, tile)

    def stored(self):
        each(self.tiles, lambda t: self.store(t).wait())


def back_chunks(m, gather, primal, wait_free):
    waves = m.full.shape[0]
    late = waves >= 4
    if not late:
        gather.forward(waves - 1)
        for w in range(max(waves - 2, 0), waves):
            gather.relay(w)

    def give(t):
        if wait_free:
            @pl.when(t == 0)
            def _():
                pl.semaphore_wait(m.free, primal.p.nw - 1)
        start(primal.exchange(t))

    def chunk(w):
        gather.arrive(w)
        m.yh[...], m.yl[...] = split(m.full[w].reshape(m.yh.shape))

        def tile(t):
            back_tile(m, w, t, primal.size)
            if late:
                pl.when((w == 0) & (t == 0))(lambda: gather.forward(waves - 1))
                pl.when((w == 1) & (t == 0))(lambda: gather.relay(waves - 2))
                pl.when((w == 2) & (t == 0))(lambda: gather.relay(waves - 1))
            pl.when(w == waves - 1)(lambda: give(t))

        each(primal.tiles, tile)

    each(waves, chunk)


def kernel(m):
    waves, u = m.full.shape[0], m.rh.shape[1]
    rows, cols = m.acc.shape
    blocks, slots = rows // BLOCK, max(1, min(2, rows // u))
    p = Place()
    gather, scatter = Gather(p, m.full, m.gather), Scatter(p, m.part, m.scatter)
    load_dual = pltpu.make_async_copy(m.dual, m.dual_v, m.local.at[0])
    load_dual.start()

    def stage(w):
        here = pl.ds(pl.multiple_of(lax.rem(w, slots) * u, u), u) if slots > 1 else pl.ds(0, u)
        return [pltpu.make_async_copy(a.at[w], b.at[here], m.stage_sems.at[w, n])
                for n, (a, b) in enumerate(((m.focal_rows, m.ext_v), (m.focal_cols, m.acc)))]

    def convert(w):
        for copy in stage(w):
            copy.wait()
        base = lax.rem(w, slots) * u
        for a, top, low in ((m.ext_v, m.rh, m.rl), (m.acc, m.ch, m.cl)):
            def part(i):
                here = pl.ds(pl.multiple_of(i * 64, 64), 64)
                top[w, here, :], low[w, here, :] = split(a[pl.ds(pl.multiple_of(base + i * 64, 64), 64), :])

            each(u // 64, part)
        pl.when(w + slots < waves)(lambda: start(stage(w + slots)))

    each(slots, lambda w: start(stage(w)))
    p.greet(True)
    for w in range(waves):
        m.full[w, p.r, p.c] = m.y[:, w, :] * m.dark[:, w, :].astype(f32)
    gather.start(0)
    for w in range(waves):
        gather.spread(w)
    halo = Halo(p, m.dual_v, m.halos[:4])
    load_dual.wait()
    halo.start()

    def advance(w):
        pl.when(w < waves - 1)(lambda: gather.forward(w, lambda: gather.start(w + 1)))
        convert(w)
        pl.when((w > 0) & (w < waves - 1))(lambda: gather.relay(w - 1))

    each(waves, advance)
    clear(m)
    halo.result(m.dual_r, m.dual_c)
    halo.finish()
    for iteration in range(ITERS):
        first, last = iteration == 0, iteration == ITERS - 1
        primal = Primal(p, m, m.x if first else m.x_mid, m.x_out if last else m.x_mid)
        primal.begin()
        back_chunks(m, gather, primal, not first)
        gather.finish()
        primal.finish()
        if not last:
            for n in range(1, p.nw):
                pl.semaphore_signal(m.free, inc=1, device_id=p.wave(n), device_id_type=MESH)
        forward_and_turn(m, p, gather, scatter, 1 + 2 * iteration, primal, first, last)


def forward_and_turn(m, p, gather, scatter, halos, primal, first, last):
    n = m.full.shape[0]
    blocks = m.ext_v.shape[0] // BLOCK
    halo = Halo(p, m.ext_v, m.halos[4 * halos:4 * halos + 4])
    halo.start()

    def result(w):
        dark = m.dark[:, w, :].astype(f32)
        old = m.y[:, w, :] * dark if first else m.y_out[:, w, :]
        new = dark * prox(old + step_dual * scatter.result(w), contrast)
        m.y_out[:, w, :] = new
        if not last:
            m.full[w, p.r, p.c] = new
            gather.start(w)
            gather.spread(w)

    def dual(lo, hi):
        curvature_step(m.dual_v, m.ext_v, m.ext_r, m.ext_c, blocks * lo // 4, blocks * hi // 4)

    def steps(*pairs):
        for step, w in pairs:
            if 0 <= w < n:
                step(w)

    def product(w):
        forward_left(m, w)
        pl.when(w >= 1)(lambda: scatter.combine(w - 1))
        pl.when(w >= 2)(lambda: scatter.column(w - 2))
        forward_part(m, w)
        scatter.start(w)

    each(n, product)
    for w in range(n - 3):
        result(w)
    halo.result(m.ext_r, m.ext_c)
    halo.finish()
    primal.stored()
    if not last:
        clear(m)
    dual(0, 1)
    steps((result, n - 3), (scatter.combine, n - 1), (scatter.column, n - 2))
    if not last:
        for w in range(n - 4):
            steps((gather.forward, w), (gather.relay, w))
        steps((gather.forward, n - 4))
    dual(1, 2)
    steps((scatter.column, n - 1), (result, n - 2))
    if not last:
        steps((gather.forward, n - 3), (gather.relay, n - 4))
    dual(2, 4)
    if last:
        store = pltpu.make_async_copy(m.dual_v, m.dual_out, m.local.at[1])
        store.start()
    else:
        halo = Halo(p, m.dual_v, m.halos[4 * halos + 4:4 * halos + 8])
        halo.start()
    steps((result, n - 1))
    if not last:
        steps((gather.forward, n - 2), (gather.relay, n - 3))
    scatter.finish()
    if last:
        store.wait()
    else:
        halo.result(m.dual_r, m.dual_c)
        halo.finish()


def call(ins, outs, scratch):
    names, flat, counts = list(ins) + list(outs), [], {}
    for name, what in scratch.items():
        counts[name] = len(what) if isinstance(what, list) else None
        flat += what if isinstance(what, list) else [what]

    def body(*refs):
        m = types.SimpleNamespace(**dict(zip(names, refs)))
        rest = list(refs[len(names):])
        for name, count in counts.items():
            setattr(m, name, [rest.pop(0) for _ in range(count)] if count is not None else rest.pop(0))
        kernel(m)

    out = pl.pallas_call(
        body,
        in_specs=[spec for _, spec in ins.values()], out_specs=[spec for _, spec in outs.values()],
        out_shape=[what for what, _ in outs.values()], scratch_shapes=flat,
        compiler_params=pltpu.CompilerParams(collective_id=0, has_side_effects=True, vmem_limit_bytes=LIMIT),
    )(*[value for value, _ in ins.values()])
    return types.SimpleNamespace(**dict(zip(outs, out)))


def per_device(transmission, dual_focal, dual_curvature, pupil_mask, lyot_mask, dark_mask, focal_rows, focal_cols):
    nr, nc, nw = lax.axis_size("row"), lax.axis_size("col"), lax.axis_size("wave")
    na = 2 if nc % 2 == 0 else 1
    nb = nc // na
    k, waves, z = dual_focal.shape
    u = focal_rows.shape[1]
    rows, cols = transmission.shape
    tile = min(512, rows)
    assert rows == cols and u <= rows and u == z, "tile shape"
    b = lambda *dims: pltpu.VMEM(dims, bf16)
    v = lambda *dims: pltpu.VMEM(dims, f32)
    scratch = dict(
        rh=b(waves, u, rows), rl=b(waves, u, rows), ch=b(waves, z, cols), cl=b(waves, z, cols), stage_sems=DMA((waves, 2)),
        ah=b(rows, cols), al=b(rows, cols), ext_v=v(rows, cols), dual_v=v(rows, cols), local=DMA((2,)),
        full=v(waves, nr, nc, k, z), part=v(waves, nr, nc, k, z), lh=b(u, cols), ll=b(u, cols), sh=b(tile, z), sl=b(tile, z),
        yh=b(u, z), yl=b(u, z), dual_r=v(2, 8, cols), dual_c=v(2, 8, rows), ext_r=v(2, 8, cols), ext_c=v(2, 8, rows),
        free=pltpu.SemaphoreType.REGULAR, gather=Gather.scratch(waves, nr, na, nb), scatter=Scatter.scratch(waves, nr, na, nb, k, z),
        halos=Halo.scratch(rows, cols) * (2 * ITERS), **Primal.scratch(rows, cols, nw, tile))
    ins = dict(
        y=(dual_focal, VMEM), dark=(dark_mask, VMEM), x=(transmission, ANY), dual=(dual_curvature, ANY), pupil=(pupil_mask, ANY),
        lyot=(lyot_mask, ANY), focal_rows=(focal_rows, ANY), focal_cols=(focal_cols, ANY))
    outs = dict(
        x_out=(shape(rows, cols), ANY), y_out=(shape(k, waves, z), VMEM), dual_out=(shape(rows, cols), ANY), x_mid=(shape(rows, cols), ANY))
    out = call(ins, outs, scratch)
    return out.x_out, out.y_out, out.dual_out


def solution(mesh):
    return jax.shard_map(
        per_device,
        mesh=mesh,
        in_specs=(
            P("row", "col"),
            P(("row", "col"), "wave", None),
            P("row", "col"),
            P("row", "col"),
            P("row", "col"),
            P(("row", "col"), "wave", None),
            P("wave", None, "row"),
            P("wave", None, "col"),
        ),
        out_specs=(P("row", "col"), P(("row", "col"), "wave", None), P("row", "col")),
        check_vma=False,
    )
```

profile of v0, /device:TPU:0, one launch (start us, length us, event | category | flops | bytes accessed | tf_op | source)
XLA Modules:
  0.0 235.7 jit_solution(11956602151110015802)
XLA Ops:
  0.6 227.4 %shard_map.103 = (f32[1024,1024]{1,0:T(8,128)}, f32[32,4,512]{2,1,0:T(4,128)}, f32[1024,1024]{1,0:T(8,128)}, f32[1024,1024]{1,0:T(8,128)}) custom-call(f32[32,4,512]{2,1,0:T(4,128)} %refs_0_.1, s32[32,4,512]{2,1,0:T(4,128)} %refs_1_.1, f32[1024,1024]{1,0:T(8,128)} %refs_2_.1, f32[1024,1024]{1,0:T(8,128)} %refs_3_.1, s32[1024,1024]{1,0:T(8,128)} %refs_4_.1, ...), custom_call_target="tpu_custom_call" | custom-call | tf_op jit(solution)/shard_map/pallas_call | solution.py:604
  228.0 0.0 copy-start.1
  228.0 0.0 copy-start
  228.0 4.9 %copy.14 = f32[1024,1024]{1,0:T(8,128)} copy(f32[1024,1024]{1,0:T(8,128)} %get-tuple-element.12) | data formatting | bytes 8388608
  232.9 0.0 copy-done.1
  233.0 0.7 copy.15
  233.7 0.0 copy-done
  233.7 2.0 copy.16
Async XLA Ops:
  228.0 5.0 %copy-start.1 = (f32[32,4,512]{2,1,0:T(4,128)S(1)}, f32[32,4,512]{2,1,0:T(4,128)}, u32[]{:S(2)}) copy-start(f32[32,4,512]{2,1,0:T(4,128)} %get-tuple-element.13) | copy-start | bytes 786436
  228.0 5.7 %copy-start = (f32[1024,1024]{1,0:T(8,128)S(1)}, f32[1024,1024]{1,0:T(8,128)}, u32[]{:S(2)}) copy-start(f32[1024,1024]{1,0:T(8,128)} %get-tuple-element.14) | copy-start | bytes 12582916
where the time goes:
time: 236 us
  Pallas kernels  227 us (96%)
  local copies, waits for them, and re-layouts  7.66 us (3%)
    pallas_call x1, Pallas kernels, call(): pl.pallas_call(body, in_specs=[spec for _, spec in ins.values()], out_spe...  227 us
    unnamed x7, local copies, waits for them, and re-layouts  7.66 us

commit v1 on v0

--- a/solution.py
+++ b/solution.py
@@ -337,7 +337,7 @@
     m.part[w] = out.reshape(m.part.shape[1:])
 
 
-def back_tile(m, w, t, size):
+def back_tile(m, w, t, size, then):
     cols = m.acc.shape[1]
     i = pl.ds(pl.multiple_of(t * size, size), size)
     m.sh[...], m.sl[...] = split(dot3((m.rh[w, :, i], m.rl[w, :, i]), (m.yh[...], m.yl[...]), ((0,), (0,))))
@@ -345,6 +345,7 @@
     for n in range(cols // step):
         j = pl.ds(n * step, step)
         m.acc[i, j] = m.acc[i, j] + dot3((m.sh[...], m.sl[...]), (m.ch[w, :, j], m.cl[w, :, j]), ((1,), (0,)))
+        then(n)
 
 
 def clear(m):
@@ -357,6 +358,8 @@
 class Primal:
     def __init__(self, p, m, x, x_out):
         self.p, self.m, self.x, self.x_out = p, m, x, x_out
+        self.width = min(512, m.acc.shape[1])
+        self.pieces = m.acc.shape[1] // self.width
         rows = m.acc.shape[0]
         self.size = m.sh.shape[0]
         self.tiles = rows // self.size
@@ -366,7 +369,7 @@
         v = lambda *dims: pltpu.VMEM(dims, f32)
         i32 = lambda *dims: pltpu.VMEM(dims, jnp.int32)
         return dict(
-            acc=v(rows, cols), other=v(max(nw - 1, 1), rows, cols), wave_sems=DMA((2, rows // tile, nw)),
+            acc=v(rows, cols), other=v(max(nw - 1, 1), rows, cols), wave_sems=DMA((2, rows // tile, nw, cols // min(512, cols))),
             x_in=v(2, BLOCK, cols), pupil_in=i32(2, BLOCK, cols), lyot_in=i32(2, BLOCK, cols), in_sems=DMA((2, 3)),
             out_sems=DMA((rows // tile,)))
 
@@ -381,10 +384,10 @@
             for copy in self.load(i, i):
                 copy.start()
 
-    def exchange(self, t):
+    def exchange(self, t, n):
         p, m = self.p, self.m
-        here = pl.ds(pl.multiple_of(t * self.size, self.size), self.size)
-        return [remote(m.acc.at[here], m.other.at[n - 1, here], m.wave_sems, (t, n), p.wave(n)) for n in range(1, p.nw)]
+        here = pl.ds(pl.multiple_of(t * self.size, self.size), self.size), pl.ds(n * self.width, self.width)
+        return [remote(m.acc.at[here], m.other.at[(e - 1,) + here], m.wave_sems, (t, e, n), p.wave(e)) for e in range(1, p.nw)]
 
     def store(self, t):
         m = self.m
@@ -419,8 +422,9 @@
         per = self.size // BLOCK
 
         def tile(t):
-            for copy in self.exchange(t):
-                copy.wait()
+            for n in range(self.pieces):
+                for copy in self.exchange(t, n):
+                    copy.wait()
             each(per, lambda i: self.step(t * per + i))
             self.store(t).start()
 
@@ -438,24 +442,23 @@
         for w in range(max(waves - 2, 0), waves):
             gather.relay(w)
 
-    def give(t):
-        if wait_free:
+    def give(t, n):
+        if wait_free and n == 0:
             @pl.when(t == 0)
             def _():
                 pl.semaphore_wait(m.free, primal.p.nw - 1)
-        start(primal.exchange(t))
+        start(primal.exchange(t, n))
 
     def chunk(w):
         gather.arrive(w)
         m.yh[...], m.yl[...] = split(m.full[w].reshape(m.yh.shape))
 
         def tile(t):
-            back_tile(m, w, t, primal.size)
+            back_tile(m, w, t, primal.size, lambda n: pl.when(w == waves - 1)(lambda: give(t, n)))
             if late:
                 pl.when((w == 0) & (t == 0))(lambda: gather.forward(waves - 1))
                 pl.when((w == 1) & (t == 0))(lambda: gather.relay(waves - 2))
                 pl.when((w == 2) & (t == 0))(lambda: gather.relay(waves - 1))
-            pl.when(w == waves - 1)(lambda: give(t))
 
         each(primal.tiles, tile)
 

time: 236 us -> 235 us (level)
  no operation moved by 1% of the time
where the time goes in v1:
time: 235 us; the launch traced here: 234 us
  Pallas kernels  226 us (96%)
  local copies, waits for them, and re-layouts  7.66 us (3%)
    pallas_call x1, Pallas kernels, call(): pl.pallas_call(body, in_specs=[spec for _, spec in ins.values()], out_spe...  226 us
    unnamed x7, local copies, waits for them, and re-layouts  7.66 us

profile of v1, /device:TPU:0, one launch (start us, length us, event | category | flops | bytes accessed | tf_op | source)
XLA Modules:
  0.0 234.3 jit_solution(13641792410734561824)
XLA Ops:
  0.6 226.0 %shard_map.103 = (f32[1024,1024]{1,0:T(8,128)}, f32[32,4,512]{2,1,0:T(4,128)}, f32[1024,1024]{1,0:T(8,128)}, f32[1024,1024]{1,0:T(8,128)}) custom-call(f32[32,4,512]{2,1,0:T(4,128)} %refs_0_.1, s32[32,4,512]{2,1,0:T(4,128)} %refs_1_.1, f32[1024,1024]{1,0:T(8,128)} %refs_2_.1, f32[1024,1024]{1,0:T(8,128)} %refs_3_.1, s32[1024,1024]{1,0:T(8,128)} %refs_4_.1, ...), custom_call_target="tpu_custom_call" | custom-call | tf_op jit(solution)/shard_map/pallas_call | solution.py:607
  226.6 0.0 copy-start.1
  226.6 0.0 copy-start
  226.6 4.9 %copy.14 = f32[1024,1024]{1,0:T(8,128)} copy(f32[1024,1024]{1,0:T(8,128)} %get-tuple-element.12) | data formatting | bytes 8388608
  231.6 0.0 copy-done.1
  231.6 0.7 copy.15
  232.3 0.0 copy-done
  232.3 2.0 copy.16
Async XLA Ops:
  226.6 5.0 %copy-start.1 = (f32[32,4,512]{2,1,0:T(4,128)S(1)}, f32[32,4,512]{2,1,0:T(4,128)}, u32[]{:S(2)}) copy-start(f32[32,4,512]{2,1,0:T(4,128)} %get-tuple-element.13) | copy-start | bytes 786436
  226.6 5.7 %copy-start = (f32[1024,1024]{1,0:T(8,128)S(1)}, f32[1024,1024]{1,0:T(8,128)}, u32[]{:S(2)}) copy-start(f32[1024,1024]{1,0:T(8,128)} %get-tuple-element.14) | copy-start | bytes 12582916

commit v2 on v1

--- a/solution.py
+++ b/solution.py
@@ -213,7 +213,7 @@
         return [remote(self.q.at[w, p.row(d)], self.gz.at[w, d], self.zs, (w, d), {"row": p.row(d)}) for d in range(1, p.nr)]
 
     def start(self, w):
-        start(self.first(w))
+        start(self.first(w) + self.direct(w))
 
     def combine(self, w):
         p = self.p
@@ -228,7 +228,7 @@
             for e in range(1, p.nb):
                 total = total + self.g1[w, f - 1, e - 1]
             self.g1[w, f - 1, 0] = total
-        start(self.second(w) + self.direct(w))
+        start(self.second(w))
 
     def column(self, w):
         p = self.p
@@ -492,9 +492,9 @@
         pl.when(w + slots < waves)(lambda: start(stage(w + slots)))
 
     each(slots, lambda w: start(stage(w)))
-    p.greet(True)
     for w in range(waves):
         m.full[w, p.r, p.c] = m.y[:, w, :] * m.dark[:, w, :].astype(f32)
+    p.greet(True)
     gather.start(0)
     for w in range(waves):
         gather.spread(w)
@@ -551,9 +551,9 @@
     def product(w):
         forward_left(m, w)
         pl.when(w >= 1)(lambda: scatter.combine(w - 1))
-        pl.when(w >= 2)(lambda: scatter.column(w - 2))
         forward_part(m, w)
         scatter.start(w)
+        pl.when(w >= 2)(lambda: scatter.column(w - 2))
 
     each(n, product)
     for w in range(n - 3):

time: 235 us -> 234 us (level)
  no operation moved by 1% of the time
where the time goes in v2:
time: 234 us
  Pallas kernels  226 us (97%)
  local copies, waits for them, and re-layouts  7.66 us (3%)
    pallas_call x1, Pallas kernels, call(): pl.pallas_call(body, in_specs=[spec for _, spec in ins.values()], out_spe...  226 us
    unnamed x7, local copies, waits for them, and re-layouts  7.66 us

profile of v2, /device:TPU:0, one launch (start us, length us, event | category | flops | bytes accessed | tf_op | source)
XLA Modules:
  0.0 234.1 jit_solution(9484349305842240455)
XLA Ops:
  0.6 225.8 %shard_map.103 = (f32[1024,1024]{1,0:T(8,128)}, f32[32,4,512]{2,1,0:T(4,128)}, f32[1024,1024]{1,0:T(8,128)}, f32[1024,1024]{1,0:T(8,128)}) custom-call(f32[32,4,512]{2,1,0:T(4,128)} %refs_0_.1, s32[32,4,512]{2,1,0:T(4,128)} %refs_1_.1, f32[1024,1024]{1,0:T(8,128)} %refs_2_.1, f32[1024,1024]{1,0:T(8,128)} %refs_3_.1, s32[1024,1024]{1,0:T(8,128)} %refs_4_.1, ...), custom_call_target="tpu_custom_call" | custom-call | tf_op jit(solution)/shard_map/pallas_call | solution.py:607
  226.4 0.0 copy-start.1
  226.4 0.0 copy-start
  226.4 4.9 %copy.14 = f32[1024,1024]{1,0:T(8,128)} copy(f32[1024,1024]{1,0:T(8,128)} %get-tuple-element.12) | data formatting | bytes 8388608
  231.4 0.0 copy-done.1
  231.4 0.7 copy.15
  232.1 0.0 copy-done
  232.1 2.0 copy.16
Async XLA Ops:
  226.4 5.0 %copy-start.1 = (f32[32,4,512]{2,1,0:T(4,128)S(1)}, f32[32,4,512]{2,1,0:T(4,128)}, u32[]{:S(2)}) copy-start(f32[32,4,512]{2,1,0:T(4,128)} %get-tuple-element.13) | copy-start | bytes 786436
  226.4 5.7 %copy-start = (f32[1024,1024]{1,0:T(8,128)S(1)}, f32[1024,1024]{1,0:T(8,128)}, u32[]{:S(2)}) copy-start(f32[1024,1024]{1,0:T(8,128)} %get-tuple-element.14) | copy-start | bytes 12582916
